TPU v7x, 512 devices: a whole 4x4x16 slice. The times are simulated.
512 devices in a mesh: row: 32 (over y_hi, z), col: 16 (over x, y_lo, core).
Axes of the slice: x: 4, y: 4 (y_hi: 2, y_lo: 2; y = y_hi * 2 + y_lo), z: 16, core: 2. Of those that a mesh axis runs over, the one named last changes fastest.
Arguments:
- incoming_evolution_embedding: bfloat16 [64, 512, 64], P(None, 'row'), may hold values from -6 to 6
- learned_affine_stretch: float32 [64], replicated, may hold values from 0.5 to 1.5
- learned_affine_offset: float32 [64], replicated, may hold values from -3 to 3
- lefthand_mapping_tensor: bfloat16 [64, 32], replicated, may hold values from -0.75 to 0.75
- righthand_mapping_tensor: bfloat16 [64, 32], replicated, may hold values from -0.75 to 0.75
- final_outer_matrix: bfloat16 [1024, 128], replicated, may hold values from -0.1875 to 0.1875
- residue_couple_cotangent: bfloat16 [512, 512, 128], P('row', 'col'), may hold values from -6 to 6
Outputs:
- alignment_gradient: bfloat16 [64, 512, 64], P('col', 'row')
- left_weight_gradient: float32 [64, 32], replicated
- right_weight_gradient: float32 [64, 32], replicated
- output_weight_gradient: float32 [1024, 128], replicated
All inputs are finite; a program needn't handle non-finite values.
Results may differ from a plain program's by a relative error of at most 0.0064.
Values may be sent and summed in bfloat16 or wider, within the bound.
No kernel may reach another device: no remote copies, remote signals or barrier semaphores. Data moves between devices by JAX's collectives and lax.ppermute only.
A program may use at most 64 MiB of HBM per device.

v0:
```python
import math
import jax
import jax.numpy as jnp
from jax import lax
from jax.sharding import PartitionSpec as P

highest = lax.Precision.HIGHEST


def broadcast(x, axis, root):
    mine = lax.axis_index(axis) == root
    return lax.psum(jnp.where(mine, x, jnp.zeros_like(x)), axis)


def standardize_features(values, learned_affine_stretch, learned_affine_offset):
    values = values.astype(jnp.float32)
    mean_value = jnp.mean(values, -1, keepdims=True)
    centred = values - mean_value
    variance = jnp.mean(centred * centred, -1, keepdims=True)
    reciprocal_spread_std = lax.rsqrt(variance + 1e-05)
    multiplied_activations = centred * reciprocal_spread_std
    standardized_activations = (
        multiplied_activations * learned_affine_stretch + learned_affine_offset
    ).astype(jnp.bfloat16)
    return (multiplied_activations, reciprocal_spread_std, standardized_activations)


def project(standardized_activations, weight):
    array_shape = standardized_activations.shape
    flat = jnp.dot(
        standardized_activations.reshape(-1, array_shape[-1]),
        weight,
        preferred_element_type=jnp.float32,
    )
    return flat.astype(jnp.bfloat16).reshape(array_shape[:-1] + (weight.shape[1],))


def outer_block(left_block, right_matrix, grad_block, final_outer_matrix, element_number, hidden):
    rows = grad_block.shape[0]
    cols = grad_block.shape[1]
    outer = lax.dot_general(
        left_block, right_matrix, (((0,), (0,)), ((), ())), preferred_element_type=jnp.float32
    )
    outer = (outer * (1.0 / element_number)).astype(jnp.bfloat16)
    outer = (
        outer.reshape(rows, hidden, cols, hidden)
        .transpose(0, 2, 1, 3)
        .reshape(rows * cols, hidden * hidden)
    )
    flat_grad = grad_block.reshape(rows * cols, grad_block.shape[2])
    weight_term = lax.dot_general(
        outer, flat_grad, (((0,), (0,)), ((), ())), preferred_element_type=jnp.float32
    )
    outer_grad = lax.dot_general(
        flat_grad, final_outer_matrix, (((1,), (1,)), ((), ())), preferred_element_type=jnp.float32
    )
    outer_grad = outer_grad.astype(jnp.bfloat16)
    outer_grad = (
        outer_grad.reshape(rows, cols, hidden, hidden)
        .transpose(0, 2, 1, 3)
        .reshape(rows * hidden, cols * hidden)
    )
    left_term = lax.dot_general(
        outer_grad, right_matrix, (((1,), (1,)), ((), ())), preferred_element_type=jnp.float32
    )
    left_term = (
        (left_term * (1.0 / element_number))
        .reshape(rows, hidden, element_number)
        .transpose(2, 0, 1)
    )
    right_term = jnp.dot(left_block, outer_grad, preferred_element_type=jnp.float32) * (
        1.0 / element_number
    )
    return (weight_term, left_term, right_term)


def norm_gradient_pass(
    left_gradient,
    right_gradient,
    lefthand_mapping_tensor,
    righthand_mapping_tensor,
    multiplied_activations,
    reciprocal_spread_std,
    learned_affine_stretch,
):
    hidden = lefthand_mapping_tensor.shape[1]
    hidden_grad = jnp.dot(
        left_gradient.reshape(-1, hidden),
        lefthand_mapping_tensor.astype(jnp.float32).T,
        precision=highest,
    )
    hidden_grad = hidden_grad + jnp.dot(
        right_gradient.reshape(-1, hidden),
        righthand_mapping_tensor.astype(jnp.float32).T,
        precision=highest,
    )
    hidden_grad = hidden_grad.reshape(multiplied_activations.shape) * learned_affine_stretch
    mean_one = jnp.mean(hidden_grad, -1, keepdims=True)
    mean_two = jnp.mean(hidden_grad * multiplied_activations, -1, keepdims=True)
    return (
        reciprocal_spread_std * (hidden_grad - mean_one - multiplied_activations * mean_two)
    ).astype(jnp.bfloat16)


def weight_grad(standardized_activations, factor_grad):
    feature_width = standardized_activations.shape[-1]
    hidden = factor_grad.shape[-1]
    return lax.dot_general(
        standardized_activations.astype(jnp.float32).reshape(-1, feature_width),
        factor_grad.reshape(-1, hidden),
        (((0,), (0,)), ((), ())),
        precision=highest,
        preferred_element_type=jnp.float32,
    )


def on_device(
    incoming_evolution_embedding,
    learned_affine_stretch,
    learned_affine_offset,
    lefthand_mapping_tensor,
    righthand_mapping_tensor,
    final_outer_matrix,
    residue_couple_cotangent,
):
    homolog_number, residue_slices, feature_width = incoming_evolution_embedding.shape
    hidden = lefthand_mapping_tensor.shape[1]
    cohort_extent = lax.axis_size("row") // lax.axis_size("col")
    residue_position = lax.axis_index("col")
    row_index = lax.axis_index("row")
    multiplied_activations, reciprocal_spread_std, standardized_activations = standardize_features(
        incoming_evolution_embedding, learned_affine_stretch, learned_affine_offset
    )
    left_factor = project(standardized_activations, lefthand_mapping_tensor)
    divide_pieces = []
    for cohort_rank in range(cohort_extent):
        divide_pieces.append(
            broadcast(
                incoming_evolution_embedding, "row", cohort_extent * residue_position + cohort_rank
            )
        )
    fetched = jnp.concatenate(divide_pieces, 1)
    fetched_normed = standardize_features(fetched, learned_affine_stretch, learned_affine_offset)[2]
    right_cols = project(fetched_normed, righthand_mapping_tensor)
    tok_cols = right_cols.shape[1]
    right_matrix = right_cols.reshape(homolog_number, tok_cols * hidden)
    block_rows = math.gcd(residue_slices, 8)
    weight_acc = jnp.zeros((hidden * hidden, final_outer_matrix.shape[1]), jnp.float32)
    right_acc = jnp.zeros((homolog_number, tok_cols * hidden), jnp.float32)
    left_parts = []
    for offset in range(0, residue_slices, block_rows):
        left_block = left_factor[:, offset : offset + block_rows, :].reshape(
            homolog_number, block_rows * hidden
        )
        grad_block = residue_couple_cotangent[offset : offset + block_rows]
        weight_term, left_term, right_term = outer_block(
            left_block, right_matrix, grad_block, final_outer_matrix, homolog_number, hidden
        )
        weight_acc = weight_acc + weight_term
        right_acc = right_acc + right_term
        left_parts.append(left_term)
    left_partial = jnp.concatenate(left_parts, 1)
    left_gradient = lax.psum_scatter(left_partial, "col", scatter_dimension=0, tiled=True)
    seq_share = homolog_number // lax.axis_size("col")
    seq_first = residue_position * seq_share
    right_partial = right_acc.reshape(homolog_number, tok_cols, hidden)
    right_total = lax.psum(right_partial, "row")
    own_part = lax.dynamic_slice_in_dim(
        right_total, row_index % cohort_extent * residue_slices, residue_slices, 1
    )
    right_rows = broadcast(own_part, "col", row_index // cohort_extent)
    right_gradient = lax.dynamic_slice_in_dim(right_rows, seq_first, seq_share, 0)
    scaled_own_part = lax.dynamic_slice_in_dim(multiplied_activations, seq_first, seq_share, 0)
    inverse_own_scale = lax.dynamic_slice_in_dim(reciprocal_spread_std, seq_first, seq_share, 0)
    normed_own = lax.dynamic_slice_in_dim(standardized_activations, seq_first, seq_share, 0)
    alignment_gradient = norm_gradient_pass(
        left_gradient,
        right_gradient,
        lefthand_mapping_tensor,
        righthand_mapping_tensor,
        scaled_own_part,
        inverse_own_scale,
        learned_affine_stretch,
    )
    left_weight = weight_grad(normed_own, left_gradient)
    right_weight = weight_grad(normed_own, right_gradient)
    out_total, left_total, right_sum = lax.psum(
        (weight_acc, left_weight, right_weight), ("row", "col")
    )
    tokens = residue_slices * lax.axis_size("row")
    return (
        alignment_gradient,
        left_total * (1.0 / tokens),
        right_sum * (1.0 / tokens),
        out_total * (1.0 / tokens),
    )


def solution(mesh):
    in_specs = (P(None, "row", None), P(), P(), P(), P(), P(), P("row", "col", None))
    out_specs = (P("col", "row", None), P(), P(), P())
    return jax.shard_map(
        on_device, mesh=mesh, in_specs=in_specs, out_specs=out_specs, check_vma=False
    )
```

profile of v0, /device:TPU:1, one launch (start us, length us, event | category | flops | bytes accessed | tf_op | source)
XLA Modules:
  0.0 1406.3 jit_solution(8164136535824600437)
XLA Ops:
  7.2 1.8 broadcast_select_fusion.1
  9.1 1.2 convert_reduce_fusion
  10.3 1.3 fusion.9
  11.7 0.3 convolution_convert_fusion.1
  12.0 0.3 copy-done.7
  12.4 0.3 convolution_convert_fusion.2
  12.7 1.6 reshape.145
  14.2 2.1 copy.62
  16.4 3.6 reshape.146
  20.0 1.1 add_convert_fusion
  21.2 0.2 convolution_convert_fusion.3
  21.3 0.2 copy.47
  21.6 0.1 copy.48
  21.7 0.2 copy-done.5
  21.9 0.5 copy-done.11
  22.3 0.9 fusion.18
  23.3 1.6 reshape.149
  24.8 2.1 copy.61
  27.0 3.6 reshape.150
  30.6 0.1 copy.49
  30.7 0.2 fusion.2
  30.9 0.2 copy.50
  31.1 1.8 copy.51
  33.0 265.5 %all-reduce.13.cloned.1.call-done = (bf16[64,16,64]{2,1,0:T(8,128)(2,1)}, bf16[64,16,64]{2,1,0:T(8,128)(2,1)}) async-done(((bf16[64,16,64]{2,1,0:T(8,128)(2,1)}, bf16[64,16,64]{2,1,0:T(8,128)(2,1)}), (bf16[64,16,64]{2,1,0:T(8,128)(2,1)}, bf16[64,16,64]{2,1,0:T(8,128)(2,1)})) %all-reduce.13.cloned.1.call-update) | async-done | bytes 262160 | tf_op jit(solution)/shard_map/psum | solution.py:12
  298.5 1.2 maximum_convert_fusion
  299.7 1.4 fusion.10
  301.2 0.6 multiply_reduce_fusion
  302.0 0.6 fusion.6
  302.6 0.3 convolution_convert_fusion
  302.8 0.3 copy.42
  303.1 0.5 reshape_reshape.3
  303.7 1.1 fusion
  304.8 1.1 fusion.1
  305.9 290.3 %all-reduce.7.cloned.1.call-done = f32[64,32,32]{2,1,0:T(8,128)} async-done(((f32[64,32,32]{2,1,0:T(8,128)}), f32[64,32,32]{2,1,0:T(8,128)}) %all-reduce.7.cloned.1.call-update) | async-done | bytes 262160 | tf_op jit(solution)/shard_map/psum | solution.py:167
  596.2 1.9 dynamic-slice_select_fusion
  598.1 0.2 all-reduce.11.cloned.1.call-start
  598.3 2.9 reshape.160
  601.2 2.1 copy.60
  603.3 3.6 reshape.161
  606.9 1.2 fusion.19
  608.0 2.8 reshape.162
  610.9 2.1 copy.59
  613.0 3.6 reshape.163
  616.7 1.2 convolution_add_fusion
  617.8 0.3 convolution_multiply_fusion.2
  618.1 0.1 copy.45
  618.3 0.3 convolution_multiply_fusion.3
  618.6 0.1 copy.43
  618.7 1.0 copy.46
  619.8 129.4 %all-reduce.9.cloned.1.call-done = f32[64,16,32]{2,1,0:T(8,128)} async-done(((f32[64,16,32]{2,1,0:T(8,128)}), f32[64,16,32]{2,1,0:T(8,128)}) %all-reduce.9.cloned.1.call-update) | async-done | bytes 131088 | tf_op jit(solution)/shard_map/psum | solution.py:12
  749.2 0.8 constant_dynamic-slice_fusion
  749.9 1.0 convolution_bitcast_fusion
  750.9 470.0 %all-reduce.11.cloned.1.call-done = f32[1024,128]{1,0:T(8,128)} async-done(((f32[1024,128]{1,0:T(8,128)}), f32[1024,128]{1,0:T(8,128)}) %all-reduce.11.cloned.1.call-update) | async-done | bytes 524304 | tf_op jit(solution)/shard_map/psum | solution.py:187
  1220.9 1.9 broadcast_multiply_fusion
  1222.8 64.8 %reduce-scatter.2.cloned.1.call-done = f32[4,16,32]{2,1,0:T(8,128)} async-done(((f32[64,16,32]{2,1,0:T(8,128)}), f32[4,16,32]{2,1,0:T(8,128)}) %reduce-scatter.2.cloned.1.call-update) | async-done | bytes 8208 | tf_op jit(solution)/shard_map/reduce_scatter | solution.py:163
  1287.6 1.0 fusion.17
  1288.6 0.2 multiply_reduce_fusion.2
  1288.9 0.9 multiply_reduce_fusion.1
  1289.7 0.7 constant_dynamic-slice_fusion.1
  1290.4 0.1 div.39
  1290.5 1.0 convolution_bitcast_fusion.1
  1291.5 106.2 %all-reduce = (f32[64,32]{0,1:T(8,128)S(1)}, f32[64,32]{0,1:T(8,128)S(1)}) all-reduce(f32[64,32]{0,1:T(8,128)S(1)} %convolution_bitcast_fusion.1, f32[64,32]{0,1:T(8,128)S(1)} %convolution_bitcast_fusion), channel_id=1, replica_groups=mesh['row'=32,'col'=16] {'row','col'}, use_global_device_ids=true, to_apply=%region_11.12 | all-reduce | flops 4096 | bytes 32768 | tf_op jit(solution)/shard_map/psum | solution.py:187
  1397.7 0.6 broadcast_multiply_fusion.3
  1398.3 1.5 multiply_convert_fusion
  (61 shorter events, 0.7 us)
Async XLA Ops:
  7.2 4.6 copy-start
  7.2 4.5 copy-start.14
  7.2 291.3 %all-reduce.13.cloned.1.call-start = ((), (), s32[]{:S(2)}) async-start(), calls=%async_computation.5 | async-start | bytes 1048576 | tf_op jit(solution)/shard_map/psum | solution.py:12
  9.1 587.1 %all-reduce.7.cloned.1.call-start = ((), (), s32[]{:S(2)}) async-start(), calls=%async_computation.2 | async-start | bytes 2097152 | tf_op jit(solution)/shard_map/psum | solution.py:167
  11.7 8.3 copy-start.13
  11.7 0.6 copy-start.7
  11.7 0.6 copy-start.9
  16.4 3.6 copy-start.1
  16.4 3.6 copy-start.17
  16.4 3.6 copy-start.20
  16.4 4.8 copy-start.15
  21.2 0.7 copy-start.5
  21.7 0.6 copy-start.11
  27.0 3.7 copy-start.6
  32.9 269.0 %copy-start.18 = (f32[64]{0:T(128)S(1)}, f32[64]{0:T(128)}, u32[]{:S(2)}) copy-start(f32[64]{0:T(128)} %param.8) | copy-start | bytes 772
  32.9 269.0 %copy-start.21 = (f32[64]{0:T(128)S(1)}, f32[64]{0:T(128)}, u32[]{:S(2)}) copy-start(f32[64]{0:T(128)} %param.9) | copy-start | bytes 772
  33.0 716.2 %all-reduce.9.cloned.1.call-start = ((), (), s32[]{:S(2)}) async-start(), calls=%async_computation.3 | async-start | bytes 1048576 | tf_op jit(solution)/shard_map/psum | solution.py:12
  298.5 2.6 copy-start.2
  298.5 2.6 copy-start.3
  298.5 4.1 copy-start.16
  301.1 2.5 copy-start.12
  598.1 622.8 %all-reduce.11.cloned.1.call-start = ((), (), s32[]{:S(2)}) async-start(), calls=%async_computation.4 | async-start | bytes 1048576 | tf_op jit(solution)/shard_map/psum | solution.py:187
  603.3 3.6 copy-start.10
  613.0 3.6 copy-start.4
  613.0 3.6 copy-start.8
  618.2 670.3 %copy-start.19 = (f32[64]{0:T(128)S(1)}, f32[64]{0:T(128)}, u32[]{:S(2)}) copy-start(f32[64]{0:T(128)} %param.8) | copy-start | bytes 772
  618.3 669.3 %reduce-scatter.2.cloned.1.call-start = ((), (), s32[]{:S(2)}) async-start(), calls=%async_computation.1 | async-start | bytes 557056 | tf_op jit(solution)/shard_map/reduce_scatter | solution.py:163
Sparse Core Ops, SparseCore 0:
  11.5 286.9 all-reduce.12
  301.4 294.7 all-reduce.6
  599.7 149.4 all-reduce.8
  754.5 466.3 all-reduce.10
  1223.5 64.0 reduce-scatter.1
where the time goes:
time: 1410 us
  waiting for transfers between devices  1220 us (87%)
  blocking collectives  106 us (8%)
  local copies, waits for them, and re-layouts  38.3 us (3%)
  other arithmetic  16.7 us (1%)
  between operations  14.3 us (1%)
    psum x1, waiting for transfers between devices, on_device(): lax.psum((weight_acc, left_weight, right_weight), ('row', 'col'))  470 us
    psum x2, waiting for transfers between devices, broadcast(): return lax.psum(jnp.where(mine, x, jnp.zeros_like(x)), axis)  395 us
    psum x1, waiting for transfers between devices, on_device(): right_total = lax.psum(right_partial, 'row')  290 us
    psum x1, blocking collectives, on_device(): lax.psum((weight_acc, left_weight, right_weight), ('row', 'col'))  106 us
    reduce_scatter x1, waiting for transfers between devices, on_device(): lax.psum_scatter(left_partial, 'col', scatter_dimension=0, tiled=True)  64.8 us
  transfers between devices with their start and end apart: 5, of which 5 were waited for; matrix products, arithmetic and copies ran while one was open for 4% of the time, Pallas kernels for 0%

commit v1 on v0

--- a/solution.py
+++ b/solution.py
@@ -185,7 +185,7 @@
     left_weight = weight_grad(normed_own, left_gradient)
     right_weight = weight_grad(normed_own, right_gradient)
     out_total, left_total, right_sum = lax.psum(
-        (weight_acc, left_weight, right_weight), ("row", "col")
+        lax.psum((weight_acc, left_weight, right_weight), "row"), "col"
     )
     tokens = residue_slices * lax.axis_size("row")
     return (

time: 1410 us -> 1060 us (0.75)
  waiting for transfers between devices: 1220 us -> 780 us
  blocking collectives: 106 us -> 198 us
    psum x1 -> x0, waiting for transfers between devices: 470 us -> none  [on_device(): lax.psum((weight_acc, left_weight, right_weight), ('row', 'col'))]
    psum x1 -> x2, blocking collectives: 106 us -> 198 us  [the longest x1 121 us: on_device(): lax.psum((weight_acc, left_weight, right_weight), 'row')]
    reduce_scatter x1, waiting for transfers between devices: 64.8 us -> 83.3 us  [on_device(): lax.psum_scatter(left_partial, 'col', scatter_dimension=0, tiled=True)]
  transfers between devices with their start and end apart: 5 -> 4, of which waited for: 5 -> 4; matrix products, arithmetic and copies ran while one was open for 4% -> 3% of each run, Pallas kernels for 0% -> 0%
where the time goes in v1:
time: 1060 us
  waiting for transfers between devices  780 us (74%)
  blocking collectives  198 us (19%)
  local copies, waits for them, and re-layouts  39.4 us (4%)
  other arithmetic  17.7 us (2%)
  between operations  14.3 us (1%)
    psum x2, waiting for transfers between devices, broadcast(): return lax.psum(jnp.where(mine, x, jnp.zeros_like(x)), axis)  402 us
    psum x1, waiting for transfers between devices, on_device(): right_total = lax.psum(right_partial, 'row')  295 us
    psum x1, blocking collectives, on_device(): lax.psum((weight_acc, left_weight, right_weight), 'row')  121 us
    reduce_scatter x1, waiting for transfers between devices, on_device(): lax.psum_scatter(left_partial, 'col', scatter_dimension=0, tiled=True)  83.3 us
    psum x1, blocking collectives, on_device(): lax.psum(lax.psum((weight_acc, left_weight, right_weight), 'row'), 'col')  77 us
  transfers between devices with their start and end apart: 4, of which 4 were waited for; matrix products, arithmetic and copies ran while one was open for 3% of the time, Pallas kernels for 0%

profile of v1, /device:TPU:1, one launch (start us, length us, event | category | flops | bytes accessed | tf_op | source)
XLA Modules:
  0.0 1059.6 jit_solution(8546771391652429842)
XLA Ops:
  7.3 1.9 broadcast_select_fusion.1
  9.2 1.2 convert_reduce_fusion
  10.4 1.3 fusion.9
  11.7 1.8 add_convert_fusion
  13.6 0.7 copy-done.3
  14.3 0.2 convolution_convert_fusion.3
  14.5 0.2 copy.47
  14.7 0.7 fusion.15
  15.3 0.1 copy.48
  15.5 0.3 convolution_convert_fusion.2
  15.8 1.6 reshape.145
  17.4 2.1 copy.62
  19.6 3.6 reshape.146
  23.1 0.3 convolution_convert_fusion.1
  23.5 0.9 fusion.18
  24.4 0.1 copy.49
  24.5 1.6 reshape.149
  26.1 2.1 copy.61
  28.3 3.6 reshape.150
  31.9 0.2 fusion.2
  32.1 0.2 copy.50
  32.3 1.8 copy.51
  34.1 264.4 %all-reduce.13.cloned.1.call-done = (bf16[64,16,64]{2,1,0:T(8,128)(2,1)}, bf16[64,16,64]{2,1,0:T(8,128)(2,1)}) async-done(((bf16[64,16,64]{2,1,0:T(8,128)(2,1)}, bf16[64,16,64]{2,1,0:T(8,128)(2,1)}), (bf16[64,16,64]{2,1,0:T(8,128)(2,1)}, bf16[64,16,64]{2,1,0:T(8,128)(2,1)})) %all-reduce.13.cloned.1.call-update) | async-done | bytes 262160 | tf_op jit(solution)/shard_map/psum | solution.py:12
  298.5 1.4 fusion.10
  299.9 1.7 multiply_reduce_fusion
  301.7 1.2 maximum_convert_fusion
  302.9 0.1 rsqrt.26
  302.9 0.6 fusion.6
  303.6 0.3 convolution_convert_fusion
  303.8 0.3 copy.42
  304.1 0.5 reshape_reshape.3
  304.7 1.1 fusion
  305.8 1.1 fusion.1
  306.8 2.8 reshape.160
  309.7 2.1 copy.60
  311.8 3.6 reshape.161
  315.4 1.2 fusion.19
  316.5 2.8 reshape.162
  319.4 2.1 copy.59
  321.6 3.6 reshape.163
  325.2 1.1 convolution_add_fusion
  326.4 0.3 convolution_multiply_fusion.3
  326.7 0.1 copy.43
  326.8 0.3 convolution_multiply_fusion.2
  327.1 0.1 copy.45
  327.2 1.0 copy.46
  328.3 294.6 %all-reduce.9.cloned.1.call-done = (f32[64,32,32]{2,1,0:T(8,128)}, f32[1024,128]{1,0:T(8,128)}) async-done(((f32[64,32,32]{2,1,0:T(8,128)}, f32[1024,128]{1,0:T(8,128)}), (f32[64,32,32]{2,1,0:T(8,128)}, f32[1024,128]{1,0:T(8,128)})) %all-reduce.9.cloned.1.call-update) | async-done | bytes 786448 | tf_op jit(solution)/shard_map/psum | solution.py:167
  622.9 1.9 dynamic-slice_select_fusion
  624.8 0.7 constant_dynamic-slice_fusion.1
  625.5 83.3 %reduce-scatter.2.cloned.1.call-done = f32[4,16,32]{2,1,0:T(8,128)} async-done(((f32[64,16,32]{2,1,0:T(8,128)}), f32[4,16,32]{2,1,0:T(8,128)}) %reduce-scatter.2.cloned.1.call-update) | async-done | bytes 8208 | tf_op jit(solution)/shard_map/reduce_scatter | solution.py:163
  708.8 1.0 convolution_bitcast_fusion.1
  709.8 1.0 fusion.17
  710.7 137.5 %all-reduce.11.cloned.1.call-done = (f32[64,16,32]{2,1,0:T(8,128)}, f32[1024,128]{1,0:T(8,128)}) async-done(((f32[64,16,32]{2,1,0:T(8,128)}, f32[1024,128]{1,0:T(8,128)}), (f32[64,16,32]{2,1,0:T(8,128)}, f32[1024,128]{1,0:T(8,128)})) %all-reduce.11.cloned.1.call-update) | async-done | bytes 655376 | tf_op jit(solution)/shard_map/psum | solution.py:12
  848.3 1.0 convolution_bitcast_fusion
  849.3 0.8 constant_dynamic-slice_fusion
  850.0 1.9 broadcast_multiply_fusion
  851.9 0.2 multiply_reduce_fusion.2
  852.1 0.1 copy.52
  852.2 0.9 multiply_reduce_fusion.1
  853.1 0.1 div.39
  853.2 120.8 %all-reduce = (f32[64,32]{0,1:T(8,128)S(1)}, f32[64,32]{0,1:T(8,128)S(1)}) all-reduce(f32[64,32]{0,1:T(8,128)S(1)} %convolution_bitcast_fusion.1, f32[64,32]{0,1:T(8,128)S(1)} %convolution_bitcast_fusion), channel_id=1, replica_groups=mesh['row'=32,'col'=16] {'row'}, use_global_device_ids=true, to_apply=%region_11.12 | all-reduce | flops 4096 | bytes 32768 | tf_op jit(solution)/shard_map/psum | solution.py:188
  973.9 77.0 %all-reduce.2 = (f32[64,32]{0,1:T(8,128)S(1)}, f32[64,32]{0,1:T(8,128)S(1)}) all-reduce(f32[64,32]{0,1:T(8,128)S(1)} %get-tuple-element.4, f32[64,32]{0,1:T(8,128)S(1)} %get-tuple-element.5), channel_id=1, replica_groups=mesh['row'=32,'col'=16] {'col'}, use_global_device_ids=true, to_apply=%region_12.13 | all-reduce | flops 4096 | bytes 32768 | tf_op jit(solution)/shard_map/psum | solution.py:187
  1051.0 0.6 broadcast_multiply_fusion.3
  1051.6 1.5 multiply_convert_fusion
  (58 shorter events, 0.5 us)
Async XLA Ops:
  7.2 8.4 copy-start
  7.2 4.5 copy-start.1
  7.2 7.1 copy-start.16
  7.2 291.3 %all-reduce.13.cloned.1.call-start = ((), (), s32[]{:S(2)}) async-start(), calls=%async_computation.4 | async-start | bytes 1048576 | tf_op jit(solution)/shard_map/psum | solution.py:12
  7.3 8.2 copy-start.15
  9.2 613.8 %all-reduce.9.cloned.1.call-start = ((), (), s32[]{:S(2)}) async-start(), calls=%async_computation.2 | async-start | bytes 3145728 | tf_op jit(solution)/shard_map/psum | solution.py:167
  11.7 1.9 copy-start.14
  13.6 0.7 copy-start.3
  15.5 8.0 copy-start.11
  15.5 4.1 copy-start.9
  15.5 7.6 copy-start.7
  19.6 4.8 copy-start.13
  24.5 7.3 copy-start.5
  28.3 3.6 copy-start.4
  32.3 270.6 %copy-start.18 = (f32[64]{0:T(128)S(1)}, f32[64]{0:T(128)}, u32[]{:S(2)}) copy-start(f32[64]{0:T(128)} %param.8) | copy-start | bytes 772
  32.3 270.6 %copy-start.20 = (f32[64]{0:T(128)S(1)}, f32[64]{0:T(128)}, u32[]{:S(2)}) copy-start(f32[64]{0:T(128)} %param.9) | copy-start | bytes 772
  299.9 3.7 copy-start.17
  302.8 1.8 copy-start.12
  302.9 2.8 copy-start.6
  311.8 3.6 copy-start.10
  321.5 3.6 copy-start.2
  321.5 3.6 copy-start.8
  326.3 382.5 %reduce-scatter.2.cloned.1.call-start = ((), (), s32[]{:S(2)}) async-start(), calls=%async_computation.1 | async-start | bytes 557056 | tf_op jit(solution)/shard_map/reduce_scatter | solution.py:163
  328.2 523.7 %copy-start.19 = (f32[64]{0:T(128)S(1)}, f32[64]{0:T(128)}, u32[]{:S(2)}) copy-start(f32[64]{0:T(128)} %param.8) | copy-start | bytes 772
  328.3 520.0 %all-reduce.11.cloned.1.call-start = ((), (), s32[]{:S(2)}) async-start(), calls=%async_computation.3 | async-start | bytes 2097152 | tf_op jit(solution)/shard_map/psum | solution.py:12
Sparse Core Ops, SparseCore 0:
  11.5 286.9 all-reduce.12
  326.5 296.4 all-reduce.8
  626.3 82.4 reduce-scatter.1
  711.6 136.6 all-reduce.10
